TPU v7x, 256 devices: a whole 4x4x8 slice. The times are simulated.
256 devices in a mesh: row: 32 (over x, z_lo, y), col: 8 (over z_hi, core).
Axes of the slice: x: 4, y: 4, z: 8 (z_hi: 4, z_lo: 2; z = z_hi * 2 + z_lo), core: 2. Of those that a mesh axis runs over, the one named last changes fastest.
Arguments:
- root_cov: float32 [6144, 6144], P('row', 'col'), as said below
- structure: int32 [16], replicated, may hold values from 0 to 47
- child_factor: float32 [2048, 4096], P('row', 'col'), may hold values from -0.9 to 0.9
- child_diag: float32 [4096, 4096], P('row', 'col'), may hold values from -6 to 6
Outputs:
- cross_cov: float32 [2048, 4096], P('row', 'col')
- child_cov: float32 [4096, 4096], P('row', 'col')
Inputs may be any that keep to these rules, and one draw needn't show every extreme that they name: root_cov is exactly symmetric and positive definite; its off-diagonal entries are small against its diagonal, which is about 1.5 times the product of a row scale and a column scale.
All inputs are finite; a program needn't handle non-finite values.
Results may differ from a plain program's by a relative error of at most 0.000078.
Values sent between devices are 32-bit elements; how exact they have to be, the bound alone decides.
No kernel may reach another device: no remote copies, remote signals or barrier semaphores. Data moves between devices by JAX's collectives and lax.ppermute only.
A program may use at most 64 MiB of HBM per device.

v0:
```python
import jax
import jax.numpy as jnp
from jax import lax
from jax.sharding import PartitionSpec as P

BLK = 128


def contract_rows(first_mat, second_mat):
    return lax.dot_general(
        first_mat,
        second_mat,
        (((0,), (0,)), ((), ())),
        precision=lax.Precision.HIGHEST,
        preferred_element_type=jnp.float32,
    )


def per_device(root_cov, structure, child_factor, child_diag):
    rows_dev = root_cov.shape[0]
    offsets = lax.iota(jnp.int32, BLK)
    struct_rows = (structure[:, None] * BLK + offsets[None, :]).reshape(-1)
    row_index = lax.axis_index("row")
    global_rows = row_index * rows_dev + lax.iota(jnp.int32, rows_dev)
    tile_index = global_rows // BLK
    rank_count = jnp.sum((structure[None, :] < tile_index[:, None]).astype(jnp.int32), axis=1)
    member = jnp.any(structure[None, :] == tile_index[:, None], axis=1)
    position = rank_count * BLK + global_rows % BLK
    shard_piece = lax.all_gather(root_cov, "col", axis=1, tiled=True)
    local_index = struct_rows
    inside = (local_index >= 0) & (local_index < shard_piece.shape[1])
    taken_rows = jnp.take(shard_piece, jnp.clip(local_index, 0, shard_piece.shape[1] - 1), axis=1)
    picked = jnp.where(inside[None, :], taken_rows, 0.0)
    shard_piece = lax.all_gather(child_factor, "row", axis=0, tiled=True)
    local_index = position
    inside = member & (local_index >= 0) & (local_index < shard_piece.shape[0])
    taken_rows = jnp.take(shard_piece, jnp.clip(local_index, 0, shard_piece.shape[0] - 1), axis=0)
    spread = jnp.where(inside[:, None], taken_rows, 0.0)
    cross_cov = lax.psum_scatter(
        -contract_rows(picked, spread), "row", scatter_dimension=0, tiled=True
    )
    factor_rows = lax.all_gather(child_factor, "col", axis=1, tiled=True)
    child_cov = child_diag + lax.psum_scatter(
        -contract_rows(factor_rows, cross_cov), "row", scatter_dimension=0, tiled=True
    )
    return (cross_cov, child_cov)


def solution(mesh):
    return jax.shard_map(
        per_device,
        mesh=mesh,
        in_specs=(P("row", "col"), P(), P("row", "col"), P("row", "col")),
        out_specs=(P("row", "col"), P("row", "col")),
        check_vma=False,
    )
```

profile of v0, /device:TPU:64, one launch (start us, length us, event | category | flops | bytes accessed | tf_op | source)
XLA Modules:
  0.0 641.2 jit_solution(759094218836384815)
XLA Ops:
  7.2 0.0 copy-start.1
  7.2 0.0 all-gather.6.cloned.1.call-start
  7.2 0.7 all-gather.6.cloned.1.call-update
  7.9 0.0 all-gather.4.cloned.1.call-start
  8.0 2.2 copy.12
  10.2 0.0 all-gather.4.cloned.1.call-update
  10.2 0.0 all-gather.8.cloned.1.call-start
  10.2 0.7 all-gather.8.cloned.1.call-update
  10.9 0.0 reduce-scatter.3.cloned.1.call-start
  11.0 0.0 copy-done.1
  11.0 0.1 convert_reduce_fusion
  11.1 0.1 compare_reduce_fusion
  11.3 0.1 compare_and_fusion
  11.4 0.1 fusion.16
  11.4 0.1 fusion.12
  11.5 160.5 %all-gather.6.cloned.1.call-done = f32[2048,512]{1,0:T(8,128)} async-done(((f32[64,512]{1,0:T(8,128)}), f32[2048,512]{1,0:T(8,128)}) %all-gather.6.cloned.1.call-update) | async-done | bytes 4194320 | tf_op jit(solution)/shard_map/all_gather | solution.py:34
  172.1 3.2 gather_fusion.1
  175.3 67.9 %all-gather.4.cloned.1.call-done = f32[192,6144]{0,1:T(8,128)} async-done(((f32[192,768]{0,1:T(8,128)}), f32[192,6144]{0,1:T(8,128)}) %all-gather.4.cloned.1.call-update) | async-done | bytes 4718608 | tf_op jit(solution)/shard_map/all_gather | solution.py:29
  243.2 9.4 %gather_fusion = f32[2048,192]{1,0:T(8,128)S(1)} fusion(f32[192,6144]{0,1:T(8,128)} %all-gather.4.cloned.1.call-done, s32[2048]{0:T(1024)S(1)} %broadcast_clamp_fusion), kind=kCustom, calls=%fused_computation | custom fusion | bytes 3153920 | tf_op jit(solution)/shard_map/jit(_take)/gather | solution.py:32
  252.7 5.3 convolution_negate_fusion
  257.9 0.0 reduce-scatter.3.cloned.1.call-update
  258.0 0.0 reduce-scatter.5.cloned.1.call-start
  258.0 14.9 %all-gather.8.cloned.1.call-done = f32[64,4096]{1,0:T(8,128)} async-done(((f32[64,512]{1,0:T(8,128)}), f32[64,4096]{1,0:T(8,128)}) %all-gather.8.cloned.1.call-update) | async-done | bytes 1048592 | tf_op jit(solution)/shard_map/all_gather | solution.py:42
  272.9 173.4 %reduce-scatter.3.cloned.1.call-done = f32[64,512]{1,0:T(8,128)} async-done(((f32[2048,512]{1,0:T(8,128)}), f32[64,512]{1,0:T(8,128)}) %reduce-scatter.3.cloned.1.call-update) | async-done | bytes 131088 | tf_op jit(solution)/shard_map/reduce_scatter | solution.py:39
  446.4 10.0 %negate_bitcast_fusion = f32[4096,512]{0,1:T(8,128)} fusion(f32[64,512]{1,0:T(8,128)} %reduce-scatter.3.cloned.1.call-done, f32[64,4096]{1,0:T(8,128)} %all-gather.8.cloned.1.call-done), kind=kOutput, calls=%fused_computation.2 | convolution fusion | flops 1612709888 | bytes 9568256 | tf_op jit(solution)/shard_map/dot_general | solution.py:10
  456.4 0.0 copy-start
  456.4 0.0 reduce-scatter.5.cloned.1.call-update
  456.5 0.9 copy-done
  457.4 0.1 copy.13
  457.5 175.3 %reduce-scatter.5.cloned.1.call-done = f32[128,512]{0,1:T(8,128)} async-done(((f32[4096,512]{0,1:T(8,128)}), f32[128,512]{0,1:T(8,128)}) %reduce-scatter.5.cloned.1.call-update) | async-done | bytes 262160 | tf_op jit(solution)/shard_map/reduce_scatter | solution.py:43
  632.9 1.0 add.152
  633.8 0.8 copy.14
  (9 shorter events, 0.1 us)
Async XLA Ops:
  7.2 3.8 copy-start.1
  7.2 164.9 %all-gather.6.cloned.1.call-start = ((), (), s32[]{:S(2)}) async-start(), calls=%async_computation.3 | async-start | bytes 4325376 | tf_op jit(solution)/shard_map/all_gather | solution.py:34
  7.9 235.3 %all-gather.4.cloned.1.call-start = ((), (), s32[]{:S(2)}) async-start(), calls=%async_computation.2 | async-start | bytes 7077888 | tf_op jit(solution)/shard_map/all_gather | solution.py:29
  10.2 262.8 %all-gather.8.cloned.1.call-start = ((), (), s32[]{:S(2)}) async-start(), calls=%async_computation.5 | async-start | bytes 1179648 | tf_op jit(solution)/shard_map/all_gather | solution.py:42
  10.9 435.5 %reduce-scatter.3.cloned.1.call-start = ((), (), s32[]{:S(2)}) async-start(), calls=%async_computation.4 | async-start | bytes 4325376 | tf_op jit(solution)/shard_map/reduce_scatter | solution.py:39
  258.0 374.9 %reduce-scatter.5.cloned.1.call-start = ((), (), s32[]{:S(2)}) async-start(), calls=%async_computation.6 | async-start | bytes 8650752 | tf_op jit(solution)/shard_map/reduce_scatter | solution.py:43
  456.4 0.9 copy-start
Sparse Core Ops, SparseCore 0:
  9.8 162.2 all-gather.5
  173.9 69.2 all-gather.3
  245.1 27.8 all-gather.7
  275.9 170.4 reduce-scatter.2
  456.6 176.2 reduce-scatter.4
where the time goes:
time: 641 us
  waiting for transfers between devices  594 us (93%)
  local copies, waits for them, and re-layouts  16.8 us (3%)
  matrix products  15.3 us (2%)
  between operations  13.9 us (2%)
    reduce_scatter x1, waiting for transfers between devices, per_device(): lax.psum_scatter(-contract_rows(factor_rows, cross_cov), 'row', scatter_d...  175 us
    reduce_scatter x1, waiting for transfers between devices, per_device(): lax.psum_scatter(-contract_rows(picked, spread), 'row', scatter_dimension...  173 us
    all_gather x1, waiting for transfers between devices, per_device(): shard_piece = lax.all_gather(child_factor, 'row', axis=0, tiled=True)  161 us
    all_gather x1, waiting for transfers between devices, per_device(): shard_piece = lax.all_gather(root_cov, 'col', axis=1, tiled=True)  67.9 us
    dot_general x2, matrix products, contract_rows(): lax.dot_general(first_mat, second_mat, (((0,), (0,)), ((), ())), precisio...  15.3 us
    all_gather x1, waiting for transfers between devices, per_device(): factor_rows = lax.all_gather(child_factor, 'col', axis=1, tiled=True)  14.9 us
  transfers between devices with their start and end apart: 5, of which 5 were waited for; matrix products, arithmetic and copies ran while one was open for 3% of the time, Pallas kernels for 0%

commit v1 on v0

--- a/solution.py
+++ b/solution.py
@@ -26,7 +26,9 @@
     rank_count = jnp.sum((structure[None, :] < tile_index[:, None]).astype(jnp.int32), axis=1)
     member = jnp.any(structure[None, :] == tile_index[:, None], axis=1)
     position = rank_count * BLK + global_rows % BLK
-    shard_piece = lax.all_gather(root_cov, "col", axis=1, tiled=True)
+    shard_piece = jnp.concatenate(
+        lax.all_to_all(jnp.stack([root_cov] * lax.axis_size("col")), "col", 0, 0), axis=1
+    )
     local_index = struct_rows
     inside = (local_index >= 0) & (local_index < shard_piece.shape[1])
     taken_rows = jnp.take(shard_piece, jnp.clip(local_index, 0, shard_piece.shape[1] - 1), axis=1)

time: 641 us -> 609 us (0.950)
  waiting for transfers between devices: 594 us -> 545 us
  starting transfers between devices: 0.2 us -> 8.37 us
  local copies, waits for them, and re-layouts: 16.8 us -> 24.4 us
    all_gather x1 -> x0, waiting for transfers between devices: 67.9 us -> none  [per_device(): shard_piece = lax.all_gather(root_cov, 'col', axis=1, tiled=True)]
    all_gather x1, waiting for transfers between devices: 161 us -> 189 us  [per_device(): shard_piece = lax.all_gather(child_factor, 'row', axis=0, tiled=True)]
    all_gather x1, waiting for transfers between devices: 14.9 us -> 5.43 us  [per_device(): factor_rows = lax.all_gather(child_factor, 'col', axis=1, tiled=True)]
    all_to_all x0 -> x1, starting transfers between devices: none -> 8.25 us  [per_device(): lax.all_to_all(jnp.stack([root_cov] * lax.axis_size('col')), 'col', 0, 0)]
  transfers between devices with their start and end apart: 5 -> 5, of which waited for: 5 -> 4; matrix products, arithmetic and copies ran while one was open for 3% -> 5% of each run, Pallas kernels for 0% -> 0%
where the time goes in v1:
time: 609 us
  waiting for transfers between devices  545 us (89%)
  local copies, waits for them, and re-layouts  24.4 us (4%)
  matrix products  15.3 us (3%)
  between operations  13.9 us (2%)
  starting transfers between devices  8.37 us (1%)
    all_gather x1, waiting for transfers between devices, per_device(): shard_piece = lax.all_gather(child_factor, 'row', axis=0, tiled=True)  189 us
    reduce_scatter x1, waiting for transfers between devices, per_device(): lax.psum_scatter(-contract_rows(factor_rows, cross_cov), 'row', scatter_d...  176 us
    reduce_scatter x1, waiting for transfers between devices, per_device(): lax.psum_scatter(-contract_rows(picked, spread), 'row', scatter_dimension...  173 us
    dot_general x2, matrix products, contract_rows(): lax.dot_general(first_mat, second_mat, (((0,), (0,)), ((), ())), precisio...  15.3 us
  transfers between devices with their start and end apart: 5, of which 4 were waited for; matrix products, arithmetic and copies ran while one was open for 5% of the time, Pallas kernels for 0%

profile of v1, /device:TPU:64, one launch (start us, length us, event | category | flops | bytes accessed | tf_op | source)
XLA Modules:
  0.0 608.8 jit_solution(9139252617354833650)
XLA Ops:
  7.2 0.0 all-gather.3.cloned.1.call-start
  7.2 0.7 all-gather.3.cloned.1.call-update
  7.9 3.7 stack.2
  11.5 0.0 copy-start.1
  11.6 8.2 %all-to-all-start = ((f32[8,192,768]{2,1,0:T(8,128)}), f32[8,192,768]{2,1,0:T(8,128)}, u32[]{:S(2)}, u32[]{:S(2)}) async-start(f32[8,192,768]{2,1,0:T(8,128)} %stack.2), calls=%async_computation | async-start | bytes 9437184 | tf_op jit(solution)/shard_map/all_to_all | solution.py:30
  19.8 0.0 all-gather.5.cloned.1.call-start
  19.8 0.7 all-gather.5.cloned.1.call-update
  20.5 0.0 reduce-scatter.3.cloned.1.call-start
  20.6 0.0 copy-done.1
  20.6 0.1 convert_reduce_fusion
  20.7 0.1 compare_reduce_fusion
  20.9 0.1 fusion.16
  21.0 0.1 compare_and_fusion
  21.0 0.1 fusion.12
  21.1 189.1 %all-gather.3.cloned.1.call-done = f32[2048,512]{1,0:T(8,128)} async-done(((f32[64,512]{1,0:T(8,128)}), f32[2048,512]{1,0:T(8,128)}) %all-gather.3.cloned.1.call-update) | async-done | bytes 4194320 | tf_op jit(solution)/shard_map/all_gather | solution.py:36
  210.2 3.2 gather_fusion.1
  213.5 0.0 all-to-all-done
  213.5 6.2 %copy.15 = f32[192,8,768]{0,2,1:T(8,128)} copy(f32[192,8,768]{2,0,1:T(8,128)} %bitcast.2) | data formatting | bytes 9437184 | tf_op jit(solution)/shard_map/reshape | solution.py:29
  219.7 9.5 %gather_fusion = f32[2048,192]{1,0:T(8,128)S(1)} fusion(f32[192,6144]{0,1:T(8,128)} %bitcast.16, s32[2048]{0:T(1024)S(1)} %broadcast_clamp_fusion), kind=kCustom, calls=%fused_computation | custom fusion | bytes 3153920 | tf_op jit(solution)/shard_map/jit(_take)/gather | solution.py:34
  229.2 5.3 convolution_negate_fusion
  234.4 0.0 reduce-scatter.3.cloned.1.call-update
  234.5 0.0 reduce-scatter.5.cloned.1.call-start
  234.5 5.4 all-gather.5.cloned.1.call-done
  239.9 173.4 %reduce-scatter.3.cloned.1.call-done = f32[64,512]{1,0:T(8,128)} async-done(((f32[2048,512]{1,0:T(8,128)}), f32[64,512]{1,0:T(8,128)}) %reduce-scatter.3.cloned.1.call-update) | async-done | bytes 131088 | tf_op jit(solution)/shard_map/reduce_scatter | solution.py:41
  413.3 10.0 %negate_bitcast_fusion = f32[4096,512]{0,1:T(8,128)} fusion(f32[64,512]{1,0:T(8,128)} %reduce-scatter.3.cloned.1.call-done, f32[64,4096]{1,0:T(8,128)} %all-gather.5.cloned.1.call-done), kind=kOutput, calls=%fused_computation.2 | convolution fusion | flops 1612709888 | bytes 9568256 | tf_op jit(solution)/shard_map/dot_general | solution.py:10
  423.3 0.0 copy-start
  423.3 0.0 reduce-scatter.5.cloned.1.call-update
  423.4 0.9 copy-done
  424.3 0.1 copy.16
  424.4 176.0 %reduce-scatter.5.cloned.1.call-done = f32[128,512]{0,1:T(8,128)} async-done(((f32[4096,512]{0,1:T(8,128)}), f32[128,512]{0,1:T(8,128)}) %reduce-scatter.5.cloned.1.call-update) | async-done | bytes 262160 | tf_op jit(solution)/shard_map/reduce_scatter | solution.py:45
  600.4 1.0 add.152
  601.4 0.8 copy.17
  (9 shorter events, 0.1 us)
Async XLA Ops:
  7.2 203.1 %all-gather.3.cloned.1.call-start = ((), (), s32[]{:S(2)}) async-start(), calls=%async_computation.3 | async-start | bytes 4325376 | tf_op jit(solution)/shard_map/all_gather | solution.py:36
  11.5 9.1 %copy-start.1 = (s32[16]{0:T(128)S(1)}, s32[16]{0:T(128)}, u32[]{:S(2)}) copy-start(s32[16]{0:T(128)} %param.5) | copy-start | bytes 196
  11.6 201.9 %all-to-all-start = ((f32[8,192,768]{2,1,0:T(8,128)}), f32[8,192,768]{2,1,0:T(8,128)}, u32[]{:S(2)}, u32[]{:S(2)}) async-start(f32[8,192,768]{2,1,0:T(8,128)} %stack.2), calls=%async_computation | async-start | bytes 9437184 | tf_op jit(solution)/shard_map/all_to_all | solution.py:30
  19.8 220.1 %all-gather.5.cloned.1.call-start = ((), (), s32[]{:S(2)}) async-start(), calls=%async_computation.5 | async-start | bytes 1179648 | tf_op jit(solution)/shard_map/all_gather | solution.py:44
  20.5 392.8 %reduce-scatter.3.cloned.1.call-start = ((), (), s32[]{:S(2)}) async-start(), calls=%async_computation.4 | async-start | bytes 4325376 | tf_op jit(solution)/shard_map/reduce_scatter | solution.py:41
  234.5 365.9 %reduce-scatter.5.cloned.1.call-start = ((), (), s32[]{:S(2)}) async-start(), calls=%async_computation.6 | async-start | bytes 8650752 | tf_op jit(solution)/shard_map/reduce_scatter | solution.py:45
  423.3 0.9 copy-start
Sparse Core Ops, SparseCore 0:
  9.8 200.3 all-gather.2
  212.1 27.8 all-gather.4
  243.1 170.2 reduce-scatter.2
  423.5 176.8 reduce-scatter.4
